TPU v7x, 32 devices: a whole 2x2x4 slice. The times are simulated.
32 devices in a mesh: groups: 2 (over y), seq: 4 (over z), head: 2 (over x), batch: 2 (over core).
Axes of the slice: x: 2, y: 2, z: 4, core: 2. Of those that a mesh axis runs over, the one named last changes fastest.
Arguments:
- queries: bfloat16 [4, 512, 2560], P(('groups', 'batch'), 'seq', 'head'), parts along dimension 0, may hold values from -6 to 6
- keys: bfloat16 [4, 512, 2560], P(('groups', 'batch'), 'seq', 'head'), parts along dimension 0, may hold values from -6 to 6
- values: bfloat16 [4, 512, 2560], P(('groups', 'batch'), 'seq', 'head'), parts along dimension 0, may hold values from -6 to 6
- cache_keys: bfloat16 [4, 8, 32, 2560], P(('groups', 'batch'), 'seq', None, 'head'), parts along dimension 0, may hold values from -6 to 6
- cache_values: bfloat16 [4, 8, 32, 2560], P(('groups', 'batch'), 'seq', None, 'head'), parts along dimension 0, may hold values from -6 to 6
- frame_list: int32 [4, 3], P(('groups', 'batch')), parts along dimension 0, may hold values from 0 to 7, as said below
- frame_place: int32 [4, 8], P(('groups', 'batch')), parts along dimension 0, may hold values from 0 to 7, each once within a row
- tile_mask: int32 [4, 4, 4], P(('groups', 'batch'), 'seq'), parts along dimension 0, may hold values from 0 to 1, as said below
Outputs:
- attention: bfloat16 [4, 512, 2560], P(('groups', 'batch'), 'seq', 'head'), parts along dimension 0
There are 2 independent parts, one for each index of `groups`. A program takes and returns all parts, laid end to end along the dimension named above; each array names one. Nothing has to cross between parts.
Inputs may be any that keep to these rules, and one draw needn't show every extreme that they name: `frame_list`: each row holds frame 0 and then 3 - 1 consecutive frame numbers. `tile_mask`: ones on the diagonal of each video's tile matrix.
All inputs are finite; a program needn't handle non-finite values.
Results may differ from a plain program's by a relative error of at most 0.006.
Values may be sent and summed in bfloat16 or wider, within the bound.
No kernel may reach another device: no remote copies, remote signals or barrier semaphores. Data moves between devices by JAX's collectives and lax.ppermute only.
A program may use at most 128 MiB of HBM per device.

v0:
```python
import math
import jax
import jax.numpy as jnp
from jax import lax
from jax.sharding import PartitionSpec as P

HD = 128
TILE = 128
NEG_FILL = -1e30


def attend(running, key_part, value_part, live, query_heads):
    videos, length, col_count = key_part.shape
    head_count = col_count // HD

    def update(previous):
        peak_old, total_old, summed_old = previous
        key_heads = key_part.reshape(videos, length, head_count, HD)
        value_heads = value_part.reshape(videos, length, head_count, HD)
        scores = jnp.einsum(
            "vqhd,vkhd->vhqk", query_heads, key_heads, preferred_element_type=jnp.float32
        ) * (1.0 / math.sqrt(HD))
        allowed = live[:, None, :, :]
        scores = jnp.where(allowed, scores, NEG_FILL)
        peak_new = jnp.maximum(peak_old, jnp.max(scores, axis=3))
        weights = jnp.where(allowed, jnp.exp(scores - peak_new[..., None]), 0.0)
        factor = jnp.exp(peak_old - peak_new)
        total_new = total_old * factor + jnp.sum(weights, axis=3)
        product = jnp.einsum(
            "vhqk,vkhd->vhqd",
            weights.astype(jnp.bfloat16),
            value_heads,
            preferred_element_type=jnp.float32,
        )
        summed_new = summed_old * factor[..., None] + product
        return (peak_new, total_new, summed_new)

    def unchanged(previous):
        return previous

    return lax.cond(jnp.any(live), update, unchanged, running)


def body(queries, keys, values, cache_keys, cache_values, frame_list, frame_place, tile_mask):
    videos, tok_rows, col_count = queries.shape
    head_count = col_count // HD
    query_heads = queries.reshape(videos, tok_rows, head_count, HD)
    running = (
        jnp.full((videos, head_count, tok_rows), NEG_FILL, jnp.float32),
        jnp.zeros((videos, head_count, tok_rows), jnp.float32),
        jnp.zeros((videos, head_count, tok_rows, HD), jnp.float32),
    )
    frame_tok = cache_keys.shape[2]
    listed = jnp.any(frame_place[:, :, None] == frame_list[:, None, :], axis=2)
    key_piece = lax.all_gather(cache_keys, "seq", axis=1, tiled=True)
    value_piece = lax.all_gather(cache_values, "seq", axis=1, tiled=True)
    count_frames = key_piece.shape[1]
    token_flags = jnp.repeat(listed, frame_tok, axis=1)
    live = jnp.broadcast_to(token_flags[:, None, :], (videos, tok_rows, count_frames * frame_tok))
    key_flat = key_piece.reshape(videos, count_frames * frame_tok, col_count)
    value_flat = value_piece.reshape(videos, count_frames * frame_tok, col_count)
    running = attend(running, key_flat, value_flat, live, query_heads)
    key_piece = lax.all_gather(keys, "seq", axis=1, tiled=True)
    value_piece = lax.all_gather(values, "seq", axis=1, tiled=True)
    length = key_piece.shape[1]
    key_tiles = jnp.arange(length, dtype=jnp.int32) // TILE
    tile_live = jnp.take(tile_mask, key_tiles, axis=2)
    running = attend(
        running, key_piece, value_piece, jnp.repeat(tile_live, TILE, axis=1) > 0, query_heads
    )
    peak, total, summed = running
    result = summed / total[..., None]
    return result.transpose(0, 2, 1, 3).reshape(videos, tok_rows, col_count).astype(jnp.bfloat16)


def solution(mesh):
    return jax.shard_map(
        body,
        mesh=mesh,
        in_specs=(
            P(("groups", "batch"), "seq", "head"),
            P(("groups", "batch"), "seq", "head"),
            P(("groups", "batch"), "seq", "head"),
            P(("groups", "batch"), "seq", None, "head"),
            P(("groups", "batch"), "seq", None, "head"),
            P(("groups", "batch"), None),
            P(("groups", "batch"), None),
            P(("groups", "batch"), "seq", None),
        ),
        out_specs=P(("groups", "batch"), "seq", "head"),
        check_vma=False,
    )
```

profile of v0, /device:TPU:0, one launch (start us, length us, event | category | flops | bytes accessed | tf_op | source)
XLA Modules:
  0.0 110.2 jit_solution(18014833076720647111)
XLA Ops:
  6.6 1.9 %copy.50 = bf16[1,128,1280]{1,2,0:T(8,128)(2,1)} copy(bf16[1,128,1280]{2,1,0:T(8,128)(2,1)} %param.13) | data formatting | bytes 655360 | tf_op args[1]
  8.6 1.9 %copy.51 = bf16[1,128,1280]{1,2,0:T(8,128)(2,1)} copy(bf16[1,128,1280]{2,1,0:T(8,128)(2,1)} %param.14) | data formatting | bytes 655360 | tf_op args[2]
  10.6 0.7 fusion.41
  11.2 2.7 %compare_select_fusion.1 = s32[512,1]{0,1:T(1,128)S(1)} fusion(s32[]{:T(128)} %bitcast.15, s32[]{:T(128)} %bitcast.16, s32[]{:T(128)} %bitcast.18, s32[]{:T(128)} %bitcast.17), kind=kLoop, calls=%fused_computation.45 | loop fusion | flops 8704 | bytes 2064 | tf_op jit(solution)/shard_map/jit(_take)/gather | solution.py:67
  14.0 0.8 broadcast_reduce_fusion
  15.6 0.1 broadcast_in_dim.89
  15.7 0.7 broadcast_reduce_fusion.1
  17.2 0.2 copy.44
  17.4 27.2 %all_gather.12 = bf16[1,8,32,1280]{3,2,0,1:T(8,128)(2,1)S(1)} all-gather(bf16[1,2,32,1280]{3,2,0,1:T(8,128)(2,1)S(1)} %bitcast.73), channel_id=1, replica_groups=mesh['groups'=2,'seq'=4,'head'=2,'batch'=2] {'seq'}, dimensions={1}, use_global_device_ids=true | all-gather | bytes 819200 | tf_op jit(solution)/shard_map/all_gather | solution.py:55
  44.6 21.8 %all_gather.13 = bf16[1,8,32,1280]{3,2,0,1:T(8,128)(2,1)S(1)} all-gather(bf16[1,2,32,1280]{3,2,0,1:T(8,128)(2,1)S(1)} %bitcast.74), channel_id=1, replica_groups=mesh['groups'=2,'seq'=4,'head'=2,'batch'=2] {'seq'}, dimensions={1}, use_global_device_ids=true | all-gather | bytes 819200 | tf_op jit(solution)/shard_map/all_gather | solution.py:56
  66.3 3.3 %conditional.2 = (f32[1,10,128]{2,1,0:T(8,128)S(1)}, f32[1,10,128]{2,1,0:T(8,128)S(1)}, f32[1,10,128,128]{3,2,1,0:T(8,128)}) conditional(s32[]{:T(128)} %convert_element_type.32, () %tuple.20, (pred[8]{0:T(512)(128)(4,1)S(1)}, bf16[1,128,10,128]{1,3,2,0:T(8,128)(2,1)S(1)}, bf16[1,8,32,1280]{3,2,0,1:T(8,128)(2,1)S(1)}, ...), branch_computations={%region_3.4_spmd, %region_4.7_spmd} | conditional | flops 170891520 | bytes 8910368 | solution.py:41
  66.3 0.4 reshape.260
  66.9 0.5 fusion.40
  67.4 0.5 fusion.3
  67.9 0.4 reshape.261
  68.3 1.3 %fusion.1 = f32[1,10,128,128]{3,2,1,0:T(8,128)} fusion(f32[10,128,256]{2,1,0:T(8,128)S(1)} %get-tuple-element.99, bf16[256,10,128]{2,1,0:T(8,128)(2,1)S(1)} %reshape.261, f32[10,128]{1,0:T(8,128)S(1)} %get-tuple-element.97, pred[256]{0:T(512)(128)(4,1)S(1)} %reshape.258, f32[10,128]{1,0:T(8,128)S(1)} %get-tuple-element.96), kind=kOutput, calls=%fused_computation.4 | convolution fusion | flops 85032960 | bytes 2631936 | tf_op jit(solution)/shard_map/cond/branch_1_fun/vhqk,vkhd->vhqd/dot_general | solution.py:29
  69.6 26.9 %all-gather.5.cloned.1.call-done = bf16[1,512,1280]{1,2,0:T(8,128)(2,1)} async-done(((bf16[1,128,1280]{1,2,0:T(8,128)(2,1)}), bf16[1,512,1280]{1,2,0:T(8,128)(2,1)}) %all-gather.5.cloned.1.call-update) | async-done | bytes 1310736 | tf_op jit(solution)/shard_map/all_gather | solution.py:64
  96.6 5.8 %conditional.3 = (f32[1,10,128]{2,1,0:T(8,128)S(1)}, f32[1,10,128,128]{2,3,1,0:T(8,128)S(1)}) conditional(s32[]{:T(128)} %convert_element_type.31, (f32[1,10,128]{2,1,0:T(8,128)S(1)}, f32[1,10,128,128]{3,2,1,0:T(8,128)}) %tuple.22, (pred[1,128,512]{2,1,0:T(8,128)(4,1)S(1)}, bf16[1,128,10,128]{1,3,2,0:T(8,128)(2,1)S(1)}, ...), branch_computations={%region_7.8_spmd, %region_8.11_spmd} | conditional | flops 344396800 | bytes 18946092 | solution.py:41
  96.6 2.0 %fusion.13 = (f32[10,128]{1,0:T(8,128)S(1)}, f32[10,128,512]{2,1,0:T(8,128)S(1)}) fusion(pred[128,512]{1,0:T(8,128)(4,1)S(1)} %bitcast.70, bf16[512,10,128]{0,2,1:T(8,128)(2,1)} %bitcast.68, bf16[1,128,10,128]{1,3,2,0:T(8,128)(2,1)S(1)} %get-tuple-element.81), kind=kOutput, calls=%fused_computation.20 | convolution fusion | flops 169736960 | bytes 4330496 | tf_op jit(solution)/shard_map/cond/branch_1_fun/vqhd,vkhd->vhqk/dot_general | solution.py:20
  98.7 0.9 fusion.15
  99.5 0.4 copy-done.4
  100.0 2.2 %fusion.26 = f32[1,10,128,128]{3,2,1,0:T(8,128)S(1)} fusion(bf16[512,10,128]{0,2,1:T(8,128)(2,1)S(1)} %bitcast.77, f32[10,128,512]{2,1,0:T(8,128)S(1)} %get-tuple-element.95, f32[10,128]{1,0:T(8,128)S(1)} %get-tuple-element.93, pred[128,512]{1,0:T(8,128)(4,1)S(1)} %bitcast.72, f32[1,10,128,128]{3,2,1,0:T(8,128)} %get-tuple-element.42, ...), kind=kOutput, calls=%fused_computation.30 | convolution fusion | flops 171376640 | bytes 5318656 | tf_op jit(solution)/shard_map/cond/branch_1_fun/vhqk,vkhd->vhqd/dot_general | solution.py:29
  102.1 0.2 copy.58
  102.4 0.9 copy.54
  (29 shorter events, 0.6 us)
Async XLA Ops:
  6.5 4.0 %copy-start.3 = (s32[1,1,4]{2,1,0:T(1,128)S(1)}, s32[1,1,4]{2,1,0:T(1,128)}, u32[]{:S(2)}) copy-start(s32[1,1,4]{2,1,0:T(1,128)} %param.19) | copy-start | bytes 52
  6.5 8.9 %copy-start.5 = (s32[1,8]{1,0:T(1,128)S(1)}, s32[1,8]{1,0:T(1,128)}, u32[]{:S(2)}) copy-start(s32[1,8]{1,0:T(1,128)} %param.18) | copy-start | bytes 100
  6.5 8.9 %copy-start.6 = (s32[1,3]{1,0:T(1,128)S(1)}, s32[1,3]{1,0:T(1,128)}, u32[]{:S(2)}) copy-start(s32[1,3]{1,0:T(1,128)} %param.17) | copy-start | bytes 40
  6.5 10.6 %copy-start = (bf16[1,128,1280]{2,1,0:T(8,128)(2,1)S(1)}, bf16[1,128,1280]{2,1,0:T(8,128)(2,1)}, u32[]{:S(2)}) copy-start(bf16[1,128,1280]{2,1,0:T(8,128)(2,1)} %param.12) | copy-start | bytes 983044
  6.5 10.8 %copy-start.1 = (bf16[1,2,32,1280]{3,2,1,0:T(8,128)(2,1)S(1)}, bf16[1,2,32,1280]{3,2,1,0:T(8,128)(2,1)}, u32[]{:S(2)}) copy-start(bf16[1,2,32,1280]{3,2,1,0:T(8,128)(2,1)} %param.15) | copy-start | bytes 491524
  6.5 63.1 %all-gather.3.cloned.1.call-start = ((), (), s32[]{:S(2)}) async-start(), calls=%async_computation | async-start | bytes 1638400 | tf_op jit(solution)/shard_map/all_gather | solution.py:63
  8.6 36.0 %copy-start.2 = (bf16[1,2,32,1280]{3,2,1,0:T(8,128)(2,1)S(1)}, bf16[1,2,32,1280]{3,2,1,0:T(8,128)(2,1)}, u32[]{:S(2)}) copy-start(bf16[1,2,32,1280]{3,2,1,0:T(8,128)(2,1)} %param.16) | copy-start | bytes 491524
  8.6 88.0 %all-gather.5.cloned.1.call-start = ((), (), s32[]{:S(2)}) async-start(), calls=%async_computation.1 | async-start | bytes 1638400 | tf_op jit(solution)/shard_map/all_gather | solution.py:64
  98.6 1.3 %copy-start.4 = (bf16[1,512,1280]{1,2,0:T(8,128)(2,1)S(1)}, bf16[1,512,1280]{1,2,0:T(8,128)(2,1)}, u32[]{:S(2)}) copy-start(bf16[1,512,1280]{1,2,0:T(8,128)(2,1)} %get-tuple-element.43) | copy-start | bytes 3932164 | tf_op jit(solution)/shard_map/cond
Sparse Core Ops, SparseCore 0:
  8.9 54.7 all-gather.2
  65.3 31.2 all-gather.4
where the time goes:
time: 111 us; the launch traced here: 110 us
  blocking collectives  49 us (44%)
  waiting for transfers between devices  27 us (24%)
  between operations  14.9 us (13%)
  local copies, waits for them, and re-layouts  7.46 us (7%)
  matrix products  5.99 us (5%)
  other arithmetic  5.75 us (5%)
    all_gather x1, blocking collectives, body(): key_piece = lax.all_gather(cache_keys, 'seq', axis=1, tiled=True)  27.2 us
    all_gather x1, waiting for transfers between devices, body(): value_piece = lax.all_gather(values, 'seq', axis=1, tiled=True)  26.9 us
    all_gather x1, blocking collectives, body(): value_piece = lax.all_gather(cache_values, 'seq', axis=1, tiled=True)  21.8 us
    unnamed x15, local copies, waits for them, and re-layouts  4.08 us
    dot_general x2, matrix products, update(): jnp.einsum('vhqk,vkhd->vhqd', weights.astype(jnp.bfloat16), value_heads,...  3.49 us
    gather x1, other arithmetic, body(): tile_live = jnp.take(tile_mask, key_tiles, axis=2)  2.7 us
    dot_general x2, matrix products, update(): jnp.einsum('vqhd,vkhd->vhqk', query_heads, key_heads, preferred_element_t...  2.5 us
  transfers between devices with their start and end apart: 2, of which 1 were waited for; matrix products, arithmetic and copies ran while one was open for 10% of the time, Pallas kernels for 0%

commit v1 on v0

--- a/solution.py
+++ b/solution.py
@@ -7,6 +7,19 @@
 HD = 128
 TILE = 128
 NEG_FILL = -1e30
+
+
+def collect(array, axis, dim):
+    ways = lax.axis_size(axis)
+    up = [(d, (d + 1) % ways) for d in range(ways)]
+    down = [(d, (d - 1) % ways) for d in range(ways)]
+    earlier, later = ([array], [array])
+    for _ in range(ways // 2):
+        earlier.append(lax.ppermute(earlier[-1], axis, up))
+    for _ in range((ways - 1) // 2):
+        later.append(lax.ppermute(later[-1], axis, down))
+    line = jnp.concatenate([*earlier[::-1], *later[1:]], axis=dim)
+    return jnp.roll(line, (lax.axis_index(axis) - ways // 2) * array.shape[dim], axis=dim)
 
 
 def attend(running, key_part, value_part, live, query_heads):
@@ -53,7 +66,7 @@
     frame_tok = cache_keys.shape[2]
     listed = jnp.any(frame_place[:, :, None] == frame_list[:, None, :], axis=2)
     key_piece = lax.all_gather(cache_keys, "seq", axis=1, tiled=True)
-    value_piece = lax.all_gather(cache_values, "seq", axis=1, tiled=True)
+    value_piece = collect(cache_values, "seq", 1)
     count_frames = key_piece.shape[1]
     token_flags = jnp.repeat(listed, frame_tok, axis=1)
     live = jnp.broadcast_to(token_flags[:, None, :], (videos, tok_rows, count_frames * frame_tok))

time: 111 us -> 106 us (0.955)
  blocking collectives: 49 us -> 24.5 us
  waiting for transfers between devices: 27 us -> 36.9 us
  starting transfers between devices: 0.08 us -> 7.8 us
  local copies, waits for them, and re-layouts: 7.46 us -> 9.65 us
    all_gather x1 -> x0, blocking collectives: 21.8 us -> none  [body(): value_piece = lax.all_gather(cache_values, 'seq', axis=1, tiled=True)]
    ppermute x0 -> x3, starting transfers between devices: none -> 7.72 us  [the longest x2 5.63 us: collect(): earlier.append(lax.ppermute(earlier[-1], axis, up))]
    all_gather x1, waiting for transfers between devices: 26.9 us -> 32 us  [body(): value_piece = lax.all_gather(values, 'seq', axis=1, tiled=True)]
    ppermute x0 -> x3, waiting for transfers between devices: none -> 4.92 us  [the longest x2 4.92 us: collect(): earlier.append(lax.ppermute(earlier[-1], axis, up))]
    all_gather x1, blocking collectives: 27.2 us -> 24.5 us  [body(): key_piece = lax.all_gather(cache_keys, 'seq', axis=1, tiled=True)]
    dynamic_slice x0 -> x1, local copies, waits for them, and re-layouts: none -> 1.13 us  [collect(): jnp.roll(line, (lax.axis_index(axis) - ways // 2) * array.shape[dim], axi...]
    unnamed x15 -> x22, local copies, waits for them, and re-layouts: 4.08 us -> 4.15 us
  transfers between devices with their start and end apart: 2 -> 5, of which waited for: 1 -> 2; matrix products, arithmetic and copies ran while one was open for 10% -> 11% of each run, Pallas kernels for 0% -> 0%
where the time goes in v1:
time: 106 us; the launch traced here: 105 us
  waiting for transfers between devices  36.9 us (35%)
  blocking collectives  24.5 us (23%)
  between operations  14.9 us (14%)
  local copies, waits for them, and re-layouts  9.65 us (9%)
  starting transfers between devices  7.8 us (7%)
  matrix products  5.99 us (6%)
  other arithmetic  5.53 us (5%)
    all_gather x1, waiting for transfers between devices, body(): value_piece = lax.all_gather(values, 'seq', axis=1, tiled=True)  32 us
    all_gather x1, blocking collectives, body(): key_piece = lax.all_gather(cache_keys, 'seq', axis=1, tiled=True)  24.5 us
    ppermute x2, starting transfers between devices, collect(): earlier.append(lax.ppermute(earlier[-1], axis, up))  5.63 us
    ppermute x2, waiting for transfers between devices, collect(): earlier.append(lax.ppermute(earlier[-1], axis, up))  4.92 us
    unnamed x22, local copies, waits for them, and re-layouts  4.15 us
    dot_general x2, matrix products, update(): jnp.einsum('vhqk,vkhd->vhqd', weights.astype(jnp.bfloat16), value_heads,...  3.49 us
    gather x1, other arithmetic, body(): tile_live = jnp.take(tile_mask, key_tiles, axis=2)  2.51 us
    dot_general x2, matrix products, update(): jnp.einsum('vqhd,vkhd->vhqk', query_heads, key_heads, preferred_element_t...  2.49 us
  transfers between devices with their start and end apart: 5, of which 2 were waited for; matrix products, arithmetic and copies ran while one was open for 11% of the time, Pallas kernels for 0%

profile of v1, /device:TPU:0, one launch (start us, length us, event | category | flops | bytes accessed | tf_op | source)
XLA Modules:
  0.0 105.4 jit_solution(15334325176263623631)
XLA Ops:
  6.6 2.0 %copy.45 = bf16[1,128,1280]{1,2,0:T(8,128)(2,1)} copy(bf16[1,128,1280]{2,1,0:T(8,128)(2,1)} %param.13) | data formatting | bytes 655360 | tf_op args[1]
  8.6 3.1 %collective-permute-start = (bf16[1,2,32,1280]{3,2,1,0:T(8,128)(2,1)}, bf16[1,2,32,1280]{3,2,1,0:T(8,128)(2,1)S(1)}, u32[]{:S(2)}, u32[]{:S(2)}) collective-permute-start(bf16[1,2,32,1280]{3,2,1,0:T(8,128)(2,1)} %param.16), channel_id=1, source_target_pairs={{0,4},{4,8},{8,12},{12,0},{1,5},{5,9},{9,13},{13,1},{2,6},{6,10},{... | collective-permute-start | bytes 491528 | tf_op jit(solution)/shard_map/ppermute | solution.py:18
  11.7 2.1 %collective-permute-start.2 = (bf16[1,2,32,1280]{3,2,1,0:T(8,128)(2,1)}, bf16[1,2,32,1280]{3,2,1,0:T(8,128)(2,1)S(1)}, u32[]{:S(2)}, u32[]{:S(2)}) collective-permute-start(bf16[1,2,32,1280]{3,2,1,0:T(8,128)(2,1)} %param.16), channel_id=1, source_target_pairs={{0,12},{4,0},{8,4},{12,8},{1,13},{5,1},{9,5},{13,9},{2,14},{6,2},{... | collective-permute-start | bytes 491528 | tf_op jit(solution)/shard_map/ppermute | solution.py:20
  13.8 1.9 %copy.46 = bf16[1,128,1280]{1,2,0:T(8,128)(2,1)} copy(bf16[1,128,1280]{2,1,0:T(8,128)(2,1)} %param.14) | data formatting | bytes 655360 | tf_op args[2]
  15.7 0.7 fusion.41
  16.4 24.5 %all_gather.9 = bf16[1,8,32,1280]{3,2,0,1:T(8,128)(2,1)S(1)} all-gather(bf16[1,2,32,1280]{3,2,0,1:T(8,128)(2,1)S(1)} %bitcast.70), channel_id=1, replica_groups=mesh['groups'=2,'seq'=4,'head'=2,'batch'=2] {'seq'}, dimensions={1}, use_global_device_ids=true | all-gather | bytes 819200 | tf_op jit(solution)/shard_map/all_gather | solution.py:68
  40.8 2.5 %compare_select_fusion.1 = s32[512,1]{0,1:T(1,128)S(1)} fusion(s32[]{:T(128)} %bitcast.14, s32[]{:T(128)} %bitcast.15, s32[]{:T(128)} %bitcast.17, s32[]{:T(128)} %bitcast.16), kind=kLoop, calls=%fused_computation.54 | loop fusion | flops 8704 | bytes 2064 | tf_op jit(solution)/shard_map/jit(_take)/gather | solution.py:80
  43.5 2.6 %collective-permute-start.1 = (bf16[1,2,32,1280]{3,2,1,0:T(8,128)(2,1)S(1)}, bf16[1,2,32,1280]{3,2,1,0:T(8,128)(2,1)S(1)}, u32[]{:S(2)}, u32[]{:S(2)}) collective-permute-start(bf16[1,2,32,1280]{3,2,1,0:T(8,128)(2,1)S(1)} %collective-permute-done), channel_id=1, source_target_pairs={{0,4},{4,8},{8,12},{12,0},{1,5},{5,9},{9,13},{13,1},{2,6},{6,10},{... | collective-permute-start | bytes 491528 | tf_op jit(solution)/shard_map/ppermute | solution.py:18
  46.0 0.8 broadcast_reduce_fusion
  47.6 0.7 broadcast_reduce_fusion.1
  49.3 4.9 %collective-permute-done.1 = bf16[1,2,32,1280]{3,2,1,0:T(8,128)(2,1)S(1)} collective-permute-done((bf16[1,2,32,1280]{3,2,1,0:T(8,128)(2,1)S(1)}, bf16[1,2,32,1280]{3,2,1,0:T(8,128)(2,1)S(1)}, u32[]{:S(2)}, u32[]{:S(2)}) %collective-permute-start.1) | collective-permute-done | bytes 163872 | tf_op jit(solution)/shard_map/ppermute | solution.py:18
  54.4 5.4 %conditional.2 = (f32[1,10,128]{2,1,0:T(8,128)S(1)}, f32[1,10,128]{2,1,0:T(8,128)S(1)}, f32[1,10,128,128]{3,2,1,0:T(8,128)}) conditional(s32[]{:T(128)} %convert_element_type.35, () %tuple.31, (pred[8,32]{1,0:T(8,128)(4,1)S(1)}, bf16[1,128,10,128]{1,3,2,0:T(8,128)(2,1)S(1)}, bf16[1,8,32,1280]{3,2,0,1:T(8,128)(2,1)S(1)}, s32[]{:T(128)}, s32[]{:T(128)}, ...), branch_computations={%region_3.4_spmd, %region_4.7_spmd} | conditional | flops 170891520 | bytes 15463891 | solution.py:54
  54.4 1.0 copy-done.1
  55.9 0.5 fusion.40
  56.4 0.5 fusion.3
  56.9 1.1 %constant_dynamic-slice_fusion = bf16[1,8,32,1280]{3,2,1,0:T(8,128)(2,1)S(1)} fusion(bf16[1,16,32,1280]{3,2,1,0:T(8,128)(2,1)} %copy-done.1, s32[]{:T(128)S(6)} %select_n.78), kind=kLoop, calls=%fused_computation.16 | loop fusion | bytes 1310724 | tf_op jit(solution)/shard_map/jit(_roll_dynamic)/dynamic_slice | solution.py:22
  58.5 1.3 %fusion.1 = f32[1,10,128,128]{3,2,1,0:T(8,128)} fusion(f32[10,128,256]{2,1,0:T(8,128)S(1)} %get-tuple-element.208, bf16[256,10,128]{2,1,0:T(8,128)(2,1)S(1)} %reshape.287, f32[10,128]{1,0:T(8,128)S(1)} %get-tuple-element.206, pred[256]{0:T(512)(128)(4,1)S(1)} %reshape.284, f32[10,128]{1,0:T(8,128)S(1)} %get-tuple-element.205), kind=kOutput, calls=%fused_computation.4 | convolution fusion | flops 85032960 | bytes 2631936 | tf_op jit(solution)/shard_map/cond/branch_1_fun/vhqk,vkhd->vhqd/dot_general | solution.py:42
  59.8 32.0 %all-gather.5.cloned.1.call-done = bf16[1,512,1280]{1,2,0:T(8,128)(2,1)} async-done(((bf16[1,128,1280]{1,2,0:T(8,128)(2,1)}), bf16[1,512,1280]{1,2,0:T(8,128)(2,1)}) %all-gather.5.cloned.1.call-update) | async-done | bytes 1310736 | tf_op jit(solution)/shard_map/all_gather | solution.py:77
  91.8 5.8 %conditional.3 = (f32[1,10,128]{2,1,0:T(8,128)S(1)}, f32[1,10,128,128]{2,3,1,0:T(8,128)S(1)}) conditional(s32[]{:T(128)} %convert_element_type.34, (f32[1,10,128]{2,1,0:T(8,128)S(1)}, f32[1,10,128,128]{3,2,1,0:T(8,128)}) %tuple.33, (pred[1,128,512]{2,1,0:T(8,128)(4,1)S(1)}, bf16[1,128,10,128]{1,3,2,0:T(8,128)(2,1)S(1)}, ...), branch_computations={%region_7.8_spmd, %region_8.11_spmd} | conditional | flops 344396800 | bytes 18946092 | solution.py:54
  91.8 2.0 %fusion.13 = (f32[10,128]{1,0:T(8,128)S(1)}, f32[10,128,512]{2,1,0:T(8,128)S(1)}) fusion(pred[128,512]{1,0:T(8,128)(4,1)S(1)} %bitcast.67, bf16[512,10,128]{0,2,1:T(8,128)(2,1)} %bitcast.65, bf16[1,128,10,128]{1,3,2,0:T(8,128)(2,1)S(1)} %get-tuple-element.188), kind=kOutput, calls=%fused_computation.21 | convolution fusion | flops 169736960 | bytes 4330496 | tf_op jit(solution)/shard_map/cond/branch_1_fun/vqhd,vkhd->vhqk/dot_general | solution.py:33
  93.9 0.9 fusion.15
  94.8 0.4 copy-done.5
  95.2 2.2 %fusion.26 = f32[1,10,128,128]{3,2,1,0:T(8,128)S(1)} fusion(bf16[512,10,128]{0,2,1:T(8,128)(2,1)S(1)} %bitcast.73, f32[10,128,512]{2,1,0:T(8,128)S(1)} %get-tuple-element.204, f32[10,128]{1,0:T(8,128)S(1)} %get-tuple-element.202, pred[128,512]{1,0:T(8,128)(4,1)S(1)} %bitcast.69, f32[1,10,128,128]{3,2,1,0:T(8,128)} %get-tuple-element.128, ...), kind=kOutput, calls=%fused_computation.31 | convolution fusion | flops 171376640 | bytes 5318656 | tf_op jit(solution)/shard_map/cond/branch_1_fun/vhqk,vkhd->vhqd/dot_general | solution.py:42
  97.7 0.9 copy.49
  (44 shorter events, 1.9 us)
Async XLA Ops:
  6.5 9.2 %copy-start.4 = (s32[1,1,4]{2,1,0:T(1,128)S(1)}, s32[1,1,4]{2,1,0:T(1,128)}, u32[]{:S(2)}) copy-start(s32[1,1,4]{2,1,0:T(1,128)} %param.19) | copy-start | bytes 52
  6.5 9.8 %copy-start.3 = (bf16[1,2,32,1280]{3,2,1,0:T(8,128)(2,1)S(1)}, bf16[1,2,32,1280]{3,2,1,0:T(8,128)(2,1)}, u32[]{:S(2)}) copy-start(bf16[1,2,32,1280]{3,2,1,0:T(8,128)(2,1)} %param.15) | copy-start | bytes 491524
  6.5 36.8 %copy-start.6 = (s32[1,8]{1,0:T(1,128)S(1)}, s32[1,8]{1,0:T(1,128)}, u32[]{:S(2)}) copy-start(s32[1,8]{1,0:T(1,128)} %param.18) | copy-start | bytes 100
  6.5 36.8 %copy-start.7 = (s32[1,3]{1,0:T(1,128)S(1)}, s32[1,3]{1,0:T(1,128)}, u32[]{:S(2)}) copy-start(s32[1,3]{1,0:T(1,128)} %param.17) | copy-start | bytes 40
  6.5 42.5 %copy-start.2 = (bf16[1,128,1280]{2,1,0:T(8,128)(2,1)S(1)}, bf16[1,128,1280]{2,1,0:T(8,128)(2,1)}, u32[]{:S(2)}) copy-start(bf16[1,128,1280]{2,1,0:T(8,128)(2,1)} %param.12) | copy-start | bytes 983044
  6.5 53.3 %all-gather.3.cloned.1.call-start = ((), (), s32[]{:S(2)}) async-start(), calls=%async_computation | async-start | bytes 1638400 | tf_op jit(solution)/shard_map/all_gather | solution.py:76
  8.6 83.2 %all-gather.5.cloned.1.call-start = ((), (), s32[]{:S(2)}) async-start(), calls=%async_computation.1 | async-start | bytes 1638400 | tf_op jit(solution)/shard_map/all_gather | solution.py:77
  8.6 34.8 %collective-permute-start = (bf16[1,2,32,1280]{3,2,1,0:T(8,128)(2,1)}, bf16[1,2,32,1280]{3,2,1,0:T(8,128)(2,1)S(1)}, u32[]{:S(2)}, u32[]{:S(2)}) collective-permute-start(bf16[1,2,32,1280]{3,2,1,0:T(8,128)(2,1)} %param.16), channel_id=1, source_target_pairs={{0,4},{4,8},{8,12},{12,0},{1,5},{5,9},{9,13},{13,1},{2,6},{6,10},{... | collective-permute-start | bytes 491528 | tf_op jit(solution)/shard_map/ppermute | solution.py:18
  11.7 42.6 %collective-permute-start.2 = (bf16[1,2,32,1280]{3,2,1,0:T(8,128)(2,1)}, bf16[1,2,32,1280]{3,2,1,0:T(8,128)(2,1)S(1)}, u32[]{:S(2)}, u32[]{:S(2)}) collective-permute-start(bf16[1,2,32,1280]{3,2,1,0:T(8,128)(2,1)} %param.16), channel_id=1, source_target_pairs={{0,12},{4,0},{8,4},{12,8},{1,13},{5,1},{9,5},{13,9},{2,14},{6,2},{... | collective-permute-start | bytes 491528 | tf_op jit(solution)/shard_map/ppermute | solution.py:20
  15.7 38.6 %copy-start = (bf16[1,2,32,1280]{3,2,1,0:T(8,128)(2,1)S(1)}, bf16[1,2,32,1280]{3,2,1,0:T(8,128)(2,1)}, u32[]{:S(2)}) copy-start(bf16[1,2,32,1280]{3,2,1,0:T(8,128)(2,1)} %param.16) | copy-start | bytes 491524
  43.5 10.7 %collective-permute-start.1 = (bf16[1,2,32,1280]{3,2,1,0:T(8,128)(2,1)S(1)}, bf16[1,2,32,1280]{3,2,1,0:T(8,128)(2,1)S(1)}, u32[]{:S(2)}, u32[]{:S(2)}) collective-permute-start(bf16[1,2,32,1280]{3,2,1,0:T(8,128)(2,1)S(1)} %collective-permute-done), channel_id=1, source_target_pairs={{0,4},{4,8},{8,12},{12,0},{1,5},{5,9},{9,13},{13,1},{2,6},{6,10},{... | collective-permute-start | bytes 491528 | tf_op jit(solution)/shard_map/ppermute | solution.py:18
  54.4 1.1 %copy-start.1 = (bf16[1,16,32,1280]{3,2,1,0:T(8,128)(2,1)}, bf16[1,16,32,1280]{3,2,1,0:T(8,128)(2,1)S(1)}, u32[]{:S(2)}) copy-start(bf16[1,16,32,1280]{3,2,1,0:T(8,128)(2,1)S(1)} %get-tuple-element.120) | copy-start | bytes 3932164 | tf_op jit(solution)/shard_map/cond
  93.9 1.3 %copy-start.5 = (bf16[1,512,1280]{1,2,0:T(8,128)(2,1)S(1)}, bf16[1,512,1280]{1,2,0:T(8,128)(2,1)}, u32[]{:S(2)}) copy-start(bf16[1,512,1280]{1,2,0:T(8,128)(2,1)} %get-tuple-element.129) | copy-start | bytes 3932164 | tf_op jit(solution)/shard_map/cond
Sparse Core Ops, SparseCore 0:
  8.9 49.2 all-gather.2
  59.8 31.9 all-gather.4
